TPU v7x, 32 devices: a whole 2x2x4 slice. The times are simulated.
32 devices in a mesh: tm: 4 (over z), tile: 2 (over y), clip: 4 (over x, core).
Axes of the slice: x: 2, y: 2, z: 4, core: 2. Of those that a mesh axis runs over, the one named last changes fastest.
Arguments:
- latents: bfloat16 [32, 16, 128, 256], P(('clip', 'tm'), 'tile'), parts along dimension 0, may hold values from -40 to 40
- norm1_gain: float32 [256], replicated, may hold values from 0.1 to 1.9
- conv1_weight: bfloat16 [27, 256, 256], P(None, None, ('tm', 'tile')), may hold values from -0.078125 to 0.078125
- conv1_bias: float32 [256], replicated, may hold values from -3 to 3
- norm2_gain: float32 [256], replicated, may hold values from 0.1 to 1.9
- conv2_weight: bfloat16 [27, 256, 256], P(None, None, ('tm', 'tile')), may hold values from -0.078125 to 0.078125
- conv2_bias: float32 [256], replicated, may hold values from -3 to 3
Outputs:
- decoded: bfloat16 [32, 16, 128, 256], P(('clip', 'tm'), 'tile'), parts along dimension 0
There are 4 independent parts, one for each index of `clip`. A program takes and returns all parts, laid end to end along the dimension named above; an argument that names none is the same for every part. Nothing has to cross between parts.
All inputs are finite; a program needn't handle non-finite values.
Results may differ from a plain program's by a relative error of at most 0.003.
Values may be sent and summed in bfloat16 or wider, within the bound.
No kernel may reach another device: no remote copies, remote signals or barrier semaphores. Data moves between devices by JAX's collectives and lax.ppermute only.
A program may use at most 64 MiB of HBM per device.

v0:
```python
import jax
import jax.numpy as jnp
from jax import lax
from jax.sharding import PartitionSpec as P

GROUPS = 32
epsilon = 1e-06


def from_behind(value, axis, steps):
    count = lax.axis_size(axis)
    first, last = (max(0, -steps), min(count, count - steps))
    return lax.ppermute(value, axis, [(source, source + steps) for source in range(first, last)])


def padded_2(block, sides, width):
    for axis, dim in sides:
        count = lax.axis_size(axis)
        forward = [(i, i + 1) for i in range(count - 1)]
        backward = [(target, source) for source, target in forward]
        low = lax.ppermute(
            lax.slice_in_dim(block, block.shape[dim] - width, None, axis=dim), axis, forward
        )
        high = lax.ppermute(lax.slice_in_dim(block, 0, width, axis=dim), axis, backward)
        block = jnp.concatenate([low, block, high], axis=dim)
    return block


def normalize(inputs_f, gain_vec):
    frames, rows_here, columns, channels = inputs_f.shape
    grouped = inputs_f.reshape(frames, rows_here * columns, GROUPS, channels // GROUPS)
    counted = float(rows_here * columns * (channels // GROUPS) * lax.axis_size("tile"))
    totals = lax.psum(jnp.sum(grouped, axis=(1, 3)), "tile")
    group_mean = totals / counted
    centered = grouped - group_mean[:, None, :, None]
    spread = lax.psum(jnp.sum(centered * centered, axis=(1, 3)), "tile")
    group_var = spread / counted
    normed = (centered * lax.rsqrt(group_var + epsilon)[:, None, :, None]).reshape(
        inputs_f.shape
    ) * gain_vec
    return jax.nn.silu(normed).astype(jnp.bfloat16)


def widen_cols(block, columns):
    padded = jnp.pad(block, ((0, 0), (0, 0), (1, 1), (0, 0)))
    return jnp.concatenate(
        [padded[:, :, shift_col : shift_col + columns] for shift_col in range(3)], axis=-1
    )


def convolve(activated, weight_shard, bias_vec):
    frames, rows_here, columns, channels = activated.shape
    cached = from_behind(activated, "tm", 1)
    extended = jnp.concatenate([cached, activated], axis=0)
    rimmed = padded_2(extended, (("tile", 1),), 1)
    shard_piece = lax.all_gather(weight_shard, ("tm", "tile"), axis=2, tiled=True)
    outputs_here = shard_piece.shape[2]
    kernel = shard_piece.reshape(3, 3, 3 * channels, outputs_here)
    summed = jnp.zeros((frames, rows_here, columns, outputs_here), jnp.float32)
    widened = widen_cols(rimmed, columns)
    for frame_off in range(3):
        for row_off in range(3):
            summed = summed + jnp.einsum(
                "trwk,kn->trwn",
                widened[frame_off : frame_off + frames, row_off : row_off + rows_here],
                kernel[frame_off, row_off],
                preferred_element_type=jnp.float32,
            )
    return summed + bias_vec


def shards(latents, norm1_gain, conv1_weight, conv1_bias, norm2_gain, conv2_weight, conv2_bias):
    inputs_f = latents.astype(jnp.float32)
    hidden = convolve(normalize(inputs_f, norm1_gain), conv1_weight, conv1_bias).astype(
        jnp.bfloat16
    )
    second = convolve(normalize(hidden.astype(jnp.float32), norm2_gain), conv2_weight, conv2_bias)
    return (inputs_f + second).astype(jnp.bfloat16)


def solution(mesh):
    placed = (
        P(("clip", "tm"), "tile", None, None),
        P(),
        P(None, None, ("tm", "tile")),
        P(),
        P(),
        P(None, None, ("tm", "tile")),
        P(),
    )
    return jax.shard_map(
        shards,
        mesh=mesh,
        in_specs=placed,
        out_specs=P(("clip", "tm"), "tile", None, None),
        check_vma=False,
    )
```

profile of v0, /device:TPU:24, one launch (start us, length us, event | category | flops | bytes accessed | tf_op | source)
XLA Modules:
  0.0 209.7 jit_solution(16347411806970437076)
XLA Ops:
  7.3 1.4 convert_reduce_fusion
  8.9 4.9 %psum.28 = f32[2,32]{1,0:T(2,128)S(1)} all-reduce(f32[2,32]{1,0:T(2,128)S(1)} %reduce_sum.51), channel_id=1, replica_groups=mesh['tm'=4,'tile'=2,'clip'=4] {'tile'}, use_global_device_ids=true, to_apply=%region_2.0 | all-reduce | flops 64 | bytes 512 | tf_op jit(solution)/shard_map/psum | solution.py:33
  14.0 1.5 fusion.15
  15.7 4.9 %psum.29 = f32[2,32]{1,0:T(2,128)S(1)} all-reduce(f32[2,32]{1,0:T(2,128)S(1)} %reduce_sum.54), channel_id=1, replica_groups=mesh['tm'=4,'tile'=2,'clip'=4] {'tile'}, use_global_device_ids=true, to_apply=%region_5.6 | all-reduce | flops 64 | bytes 512 | tf_op jit(solution)/shard_map/psum | solution.py:36
  20.8 1.3 fusion.22
  22.2 1.3 collective-permute-start
  23.5 48.3 %collective-permute-done = bf16[2,8,128,256]{3,2,1,0:T(8,128)(2,1)S(1)} collective-permute-done((bf16[2,8,128,256]{3,2,1,0:T(8,128)(2,1)S(1)}, bf16[2,8,128,256]{3,2,1,0:T(8,128)(2,1)S(1)}, u32[]{:S(2)}, u32[]{:S(2)}) %collective-permute-start) | collective-permute-done | bytes 1048608 | tf_op jit(solution)/shard_map/ppermute | solution.py:13
  72.6 3.4 %collective-permute-start.1 = (bf16[4,1,128,256]{3,2,1,0:T(8,128)(2,1)}, bf16[4,1,128,256]{3,2,1,0:T(8,128)(2,1)S(1)}, u32[]{:S(2)}, u32[]{:S(2)}) collective-permute-start(bf16[4,1,128,256]{3,2,1,0:T(8,128)(2,1)} %get-tuple-element.11), channel_id=1, source_target_pairs={{0,4},{1,5},{2,6},{3,7},{8,12},{9,13},{10,14},{11,15},{16,20},{17,... | collective-permute-start | bytes 786440 | tf_op jit(solution)/shard_map/ppermute | solution.py:21
  76.0 1.3 collective-permute-start.2
  77.3 2.8 %collective-permute-done.1 = bf16[4,1,128,256]{3,2,1,0:T(8,128)(2,1)S(1)} collective-permute-done((bf16[4,1,128,256]{3,2,1,0:T(8,128)(2,1)}, bf16[4,1,128,256]{3,2,1,0:T(8,128)(2,1)S(1)}, u32[]{:S(2)}, u32[]{:S(2)}) %collective-permute-start.1) | collective-permute-done | bytes 262176 | tf_op jit(solution)/shard_map/ppermute | solution.py:21
  80.2 4.4 %collective-permute-done.2 = bf16[4,1,128,256]{3,2,1,0:T(8,128)(2,1)} collective-permute-done((bf16[4,1,128,256]{3,2,1,0:T(8,128)(2,1)}, bf16[4,1,128,256]{3,2,1,0:T(8,128)(2,1)}, u32[]{:S(2)}, u32[]{:S(2)}) %collective-permute-start.2) | collective-permute-done | bytes 262176 | tf_op jit(solution)/shard_map/ppermute | solution.py:24
  84.6 2.1 %fusion.8 = bf16[4,10,130,256]{3,2,1,0:T(8,128)(2,1)S(1)} fusion(bf16[4,1,128,256]{3,2,1,0:T(8,128)(2,1)} %collective-permute-done.2, bf16[4,1,128,256]{3,2,1,0:T(8,128)(2,1)S(1)} %collective-permute-done.1, bf16[2,8,128,256]{3,2,1,0:T(8,128)(2,1)S(1)} %fusion.22, bf16[2,8,128,256]{3,2,1,0:T(8,128)(2,1)S(1)} %collective-permute-done), kind=kLoop, calls=%fused_computation.17 | loop fusion | flops 19968000 | bytes 5283840 | tf_op jit(solution)/shard_map/concatenate | solution.py:25
  86.7 1.9 fusion.49
  88.6 4.7 %pad_maximum_fusion = bf16[4,10,128,768]{3,2,1,0:T(8,128)(2,1)} fusion(bf16[4,10,128,256]{3,2,1,0:T(8,128)(2,1)S(1)} %get-tuple-element.8, bf16[4,1,128,256]{3,2,1,0:T(8,128)(2,1)} %collective-permute-done.2, bf16[2,8,128,256]{3,2,1,0:T(8,128)(2,1)S(1)} %fusion.22, bf16[2,8,128,256]{3,2,1,0:T(8,128)(2,1)S(1)} %collective-permute-done, ...), kind=kLoop, calls=%fused_computation.2 | loop fusion | flops 47185920 | bytes 15728640 | tf_op jit(solution)/shard_map/concatenate | solution.py:46
  93.3 5.8 %copy.10 = bf16[27,256,256]{2,1,0:T(8,128)(2,1)} copy(bf16[27,256,256]{1,2,0:T(8,128)(2,1)} %all-gather.3.cloned.1.call-done) | data formatting | bytes 7077888 | tf_op jit(solution)/shard_map/all_gather | solution.py:56
  99.0 3.1 %fusion.40 = f32[2,8,128,256]{3,2,1,0:T(8,128)S(1)} fusion(bf16[4,10,128,768]{3,2,1,0:T(8,128)(2,1)} %pad_maximum_fusion, bf16[3,3,768,256]{3,2,1,0:T(8,128)(2,1)} %bitcast.157), kind=kOutput, calls=%fused_computation.63 | convolution fusion | flops 805306368 | bytes 10354688 | tf_op jit(solution)/shard_map/trwk,kn->trwn/dot_general | solution.py:63
  102.2 3.7 %fusion.41 = f32[2,8,128,256]{3,2,1,0:T(8,128)S(1)} fusion(bf16[4,10,128,768]{3,2,1,0:T(8,128)(2,1)} %pad_maximum_fusion, bf16[3,3,768,256]{3,2,1,0:T(8,128)(2,1)S(1)} %bitcast.158), kind=kOutput, calls=%fused_computation.65 | convolution fusion | flops 805306368 | bytes 10354688 | tf_op jit(solution)/shard_map/trwk,kn->trwn/dot_general | solution.py:63
  111.9 1.5 convert_reduce_fusion.1
  113.6 5.1 %psum.30 = f32[2,32]{1,0:T(2,128)S(1)} all-reduce(f32[2,32]{1,0:T(2,128)S(1)} %reduce_sum.72), channel_id=1, replica_groups=mesh['tm'=4,'tile'=2,'clip'=4] {'tile'}, use_global_device_ids=true, to_apply=%region_8.9 | all-reduce | flops 64 | bytes 512 | tf_op jit(solution)/shard_map/psum | solution.py:33
  119.3 4.9 %psum.31 = f32[2,32]{1,0:T(2,128)S(1)} all-reduce(f32[2,32]{1,0:T(2,128)S(1)} %reduce_sum.75), channel_id=1, replica_groups=mesh['tm'=4,'tile'=2,'clip'=4] {'tile'}, use_global_device_ids=true, to_apply=%region_11.12 | all-reduce | flops 64 | bytes 512 | tf_op jit(solution)/shard_map/psum | solution.py:36
  125.1 1.3 collective-permute-start.3
  126.4 46.1 %collective-permute-done.3 = bf16[2,8,128,256]{3,2,1,0:T(8,128)(2,1)S(1)} collective-permute-done((bf16[2,8,128,256]{3,2,1,0:T(8,128)(2,1)S(1)}, bf16[2,8,128,256]{3,2,1,0:T(8,128)(2,1)S(1)}, u32[]{:S(2)}, u32[]{:S(2)}) %collective-permute-start.3) | collective-permute-done | bytes 1048608 | tf_op jit(solution)/shard_map/ppermute | solution.py:13
  173.4 3.4 %collective-permute-start.4 = (bf16[4,1,128,256]{3,2,1,0:T(8,128)(2,1)}, bf16[4,1,128,256]{3,2,1,0:T(8,128)(2,1)S(1)}, u32[]{:S(2)}, u32[]{:S(2)}) collective-permute-start(bf16[4,1,128,256]{3,2,1,0:T(8,128)(2,1)} %get-tuple-element.9), channel_id=1, source_target_pairs={{0,4},{1,5},{2,6},{3,7},{8,12},{9,13},{10,14},{11,15},{16,20},{17,... | collective-permute-start | bytes 786440 | tf_op jit(solution)/shard_map/ppermute | solution.py:21
  176.7 1.3 collective-permute-start.5
  178.1 5.7 %copy.11 = bf16[27,256,256]{2,1,0:T(8,128)(2,1)} copy(bf16[27,256,256]{1,2,0:T(8,128)(2,1)} %all-gather.5.cloned.1.call-done) | data formatting | bytes 7077888 | tf_op jit(solution)/shard_map/all_gather | solution.py:56
  183.8 2.0 collective-permute-done.5
  185.8 2.1 %select_maximum_fusion = bf16[4,10,130,256]{3,2,1,0:T(8,128)(2,1)S(1)} fusion(bf16[4,1,128,256]{3,2,1,0:T(8,128)(2,1)} %collective-permute-done.5, bf16[4,1,128,256]{3,2,1,0:T(8,128)(2,1)S(1)} %collective-permute-done.4, bf16[2,8,128,256]{3,2,1,0:T(8,128)(2,1)S(1)} %fusion.30, bf16[2,8,128,256]{3,2,1,0:T(8,128)(2,1)S(1)} %collective-permute-done.3), kind=kLoop, calls=%fused_computation.8 | loop fusion | flops 19968000 | bytes 5283840 | tf_op jit(solution)/shard_map/concatenate | solution.py:25
  187.9 1.9 fusion.48
  189.8 2.4 %pad_maximum_fusion.1 = bf16[4,10,128,768]{3,2,1,0:T(8,128)(2,1)S(1)} fusion(bf16[4,10,128,256]{3,2,1,0:T(8,128)(2,1)S(1)} %get-tuple-element.6, bf16[4,1,128,256]{3,2,1,0:T(8,128)(2,1)} %collective-permute-done.5, bf16[2,8,128,256]{3,2,1,0:T(8,128)(2,1)S(1)} %fusion.30, bf16[2,8,128,256]{3,2,1,0:T(8,128)(2,1)S(1)} %collective-permute-done.3, ...), kind=kLoop, calls=%fused_computation.3 | loop fusion | flops 47185920 | bytes 15728640 | tf_op jit(solution)/shard_map/concatenate | solution.py:46
  197.2 1.0 fusion.37
  198.2 1.0 fusion.38
  200.2 2.6 %fusion.31 = bf16[2,8,128,256]{3,2,1,0:T(8,128)(2,1)} fusion(bf16[2,8,128,256]{3,2,1,0:T(8,128)(2,1)S(1)} %copy-done.1, f32[2,8,128,256]{3,2,1,0:T(8,128)S(1)} %fusion.32, f32[2,8,128,256]{3,2,1,0:T(8,128)S(1)} %fusion.33, f32[2,8,128,256]{3,2,1,0:T(8,128)S(1)} %fusion.34, f32[2,8,128,256]{3,2,1,0:T(8,128)S(1)} %fusion.35, ...), kind=kOutput, calls=%fused_computation.42 | convolution fusion | flops 811597824 | bytes 27132928 | tf_op jit(solution)/shard_map/trwk,kn->trwn/dot_general | solution.py:63
  (57 shorter events, 16.6 us)
Async XLA Ops:
  6.5 14.3 %copy-start.1 = (bf16[2,8,128,256]{3,2,1,0:T(8,128)(2,1)S(1)}, bf16[2,8,128,256]{3,2,1,0:T(8,128)(2,1)}, u32[]{:S(2)}) copy-start(bf16[2,8,128,256]{3,2,1,0:T(8,128)(2,1)} %param.7) | copy-start | bytes 3145732
  6.5 86.7 %all-gather.3.cloned.1.call-start = ((), (), s32[]{:S(2)}) async-start(), calls=%async_computation | async-start | bytes 3981312 | tf_op jit(solution)/shard_map/all_gather | solution.py:56
  7.3 170.8 %all-gather.5.cloned.1.call-start = ((), (), s32[]{:S(2)}) async-start(), calls=%async_computation.1 | async-start | bytes 3981312 | tf_op jit(solution)/shard_map/all_gather | solution.py:56
  22.2 49.6 %collective-permute-start = (bf16[2,8,128,256]{3,2,1,0:T(8,128)(2,1)S(1)}, bf16[2,8,128,256]{3,2,1,0:T(8,128)(2,1)S(1)}, u32[]{:S(2)}, u32[]{:S(2)}) collective-permute-start(bf16[2,8,128,256]{3,2,1,0:T(8,128)(2,1)S(1)} %fusion.22), channel_id=1, source_target_pairs={{0,8},{8,16},{16,24},{1,9},{9,17},{17,25},{2,10},{10,18},{18,26},{... | collective-permute-start | bytes 3145736 | tf_op jit(solution)/shard_map/ppermute | solution.py:13
  72.6 7.6 %collective-permute-start.1 = (bf16[4,1,128,256]{3,2,1,0:T(8,128)(2,1)}, bf16[4,1,128,256]{3,2,1,0:T(8,128)(2,1)S(1)}, u32[]{:S(2)}, u32[]{:S(2)}) collective-permute-start(bf16[4,1,128,256]{3,2,1,0:T(8,128)(2,1)} %get-tuple-element.11), channel_id=1, source_target_pairs={{0,4},{1,5},{2,6},{3,7},{8,12},{9,13},{10,14},{11,15},{16,20},{17,... | collective-permute-start | bytes 786440 | tf_op jit(solution)/shard_map/ppermute | solution.py:21
  76.0 8.6 %collective-permute-start.2 = (bf16[4,1,128,256]{3,2,1,0:T(8,128)(2,1)}, bf16[4,1,128,256]{3,2,1,0:T(8,128)(2,1)}, u32[]{:S(2)}, u32[]{:S(2)}) collective-permute-start(bf16[4,1,128,256]{3,2,1,0:T(8,128)(2,1)} %get-tuple-element.12), channel_id=1, source_target_pairs={{4,0},{5,1},{6,2},{7,3},{12,8},{13,9},{14,10},{15,11},{20,16},{21,... | collective-permute-start | bytes 786440 | tf_op jit(solution)/shard_map/ppermute | solution.py:24
  99.0 3.1 %copy-start.3 = (bf16[27,256,256]{2,1,0:T(8,128)(2,1)S(1)}, bf16[27,256,256]{2,1,0:T(8,128)(2,1)}, u32[]{:S(2)}) copy-start(bf16[27,256,256]{2,1,0:T(8,128)(2,1)} %copy.10) | copy-start | bytes 10616836
  99.0 6.8 %copy-start = (bf16[4,10,128,768]{3,2,1,0:T(8,128)(2,1)S(1)}, bf16[4,10,128,768]{3,2,1,0:T(8,128)(2,1)}, u32[]{:S(2)}) copy-start(bf16[4,10,128,768]{3,2,1,0:T(8,128)(2,1)} %pad_maximum_fusion) | copy-start | bytes 23592964
  110.8 1.0 copy-start.4
  111.8 12.6 %copy-start.6 = (f32[256]{0:T(256)S(1)}, f32[256]{0:T(256)}, u32[]{:S(2)}) copy-start(f32[256]{0:T(256)} %param.11) | copy-start | bytes 3076
  125.1 47.4 %collective-permute-start.3 = (bf16[2,8,128,256]{3,2,1,0:T(8,128)(2,1)S(1)}, bf16[2,8,128,256]{3,2,1,0:T(8,128)(2,1)S(1)}, u32[]{:S(2)}, u32[]{:S(2)}) collective-permute-start(bf16[2,8,128,256]{3,2,1,0:T(8,128)(2,1)S(1)} %fusion.30), channel_id=1, source_target_pairs={{0,8},{8,16},{16,24},{1,9},{9,17},{17,25},{2,10},{10,18},{18,26},{... | collective-permute-start | bytes 3145736 | tf_op jit(solution)/shard_map/ppermute | solution.py:13
  173.4 10.5 %collective-permute-start.4 = (bf16[4,1,128,256]{3,2,1,0:T(8,128)(2,1)}, bf16[4,1,128,256]{3,2,1,0:T(8,128)(2,1)S(1)}, u32[]{:S(2)}, u32[]{:S(2)}) collective-permute-start(bf16[4,1,128,256]{3,2,1,0:T(8,128)(2,1)} %get-tuple-element.9), channel_id=1, source_target_pairs={{0,4},{1,5},{2,6},{3,7},{8,12},{9,13},{10,14},{11,15},{16,20},{17,... | collective-permute-start | bytes 786440 | tf_op jit(solution)/shard_map/ppermute | solution.py:21
  176.7 9.1 %collective-permute-start.5 = (bf16[4,1,128,256]{3,2,1,0:T(8,128)(2,1)}, bf16[4,1,128,256]{3,2,1,0:T(8,128)(2,1)}, u32[]{:S(2)}, u32[]{:S(2)}) collective-permute-start(bf16[4,1,128,256]{3,2,1,0:T(8,128)(2,1)} %get-tuple-element.10), channel_id=1, source_target_pairs={{4,0},{5,1},{6,2},{7,3},{12,8},{13,9},{14,10},{15,11},{20,16},{21,... | collective-permute-start | bytes 786440 | tf_op jit(solution)/shard_map/ppermute | solution.py:24
  189.8 2.4 %copy-start.2 = (bf16[27,256,256]{2,1,0:T(8,128)(2,1)S(1)}, bf16[27,256,256]{2,1,0:T(8,128)(2,1)}, u32[]{:S(2)}) copy-start(bf16[27,256,256]{2,1,0:T(8,128)(2,1)} %copy.11) | copy-start | bytes 10616836
  199.2 1.0 copy-start.5
Sparse Core Ops, SparseCore 0:
  9.5 76.6 all-gather.2
  88.4 73.8 all-gather.4
where the time goes:
time: 210 us
  waiting for transfers between devices  104 us (50%)
  matrix products  24.7 us (12%)
  blocking collectives  19.9 us (9%)
  other arithmetic  18.6 us (9%)
  local copies, waits for them, and re-layouts  16.3 us (8%)
  between operations  13.8 us (7%)
  starting transfers between devices  12 us (6%)
    ppermute x2, waiting for transfers between devices, from_behind(): lax.ppermute(value, axis, [(source, source + steps) for source in range(f...  94.4 us
    dot_general x18, matrix products, convolve(): jnp.einsum('trwk,kn->trwn', widened[frame_off:frame_off + frames, row_off...  24.7 us
    all_gather x2, local copies, waits for them, and re-layouts, convolve(): lax.all_gather(weight_shard, ('tm', 'tile'), axis=2, tiled=True)  11.5 us
    psum x2, blocking collectives, normalize(): totals = lax.psum(jnp.sum(grouped, axis=(1, 3)), 'tile')  10 us
    psum x2, blocking collectives, normalize(): spread = lax.psum(jnp.sum(centered * centered, axis=(1, 3)), 'tile')  9.86 us
    concatenate x2, other arithmetic, widen_cols(): jnp.concatenate([padded[:, :, shift_col:shift_col + columns] for shift_co...  7.11 us
    ppermute x2, starting transfers between devices, padded_2(): lax.ppermute(lax.slice_in_dim(block, block.shape[dim] - width, None, axis...  6.77 us
    ppermute x2, waiting for transfers between devices, padded_2(): lax.ppermute(lax.slice_in_dim(block, 0, width, axis=dim), axis, backward)  6.4 us
  transfers between devices with their start and end apart: 8, of which 5 were waited for; matrix products, arithmetic and copies ran while one was open for 20% of the time, Pallas kernels for 0%

commit v1 on v0

--- a/solution.py
+++ b/solution.py
@@ -53,7 +53,23 @@
     cached = from_behind(activated, "tm", 1)
     extended = jnp.concatenate([cached, activated], axis=0)
     rimmed = padded_2(extended, (("tile", 1),), 1)
-    shard_piece = lax.all_gather(weight_shard, ("tm", "tile"), axis=2, tiled=True)
+    t_next = lax.axis_size(("tm", "tile"))
+    shaped, right_arr, ready = (t_next, lax.axis_index(("tm", "tile")), weight_shard.shape[2])
+    all_values, t1 = (weight_shard, 1)
+    while t1 < shaped:
+        all_values = jnp.concatenate(
+            [
+                all_values,
+                lax.ppermute(
+                    all_values,
+                    ("tm", "tile"),
+                    tuple(((w, (w - t1) % shaped) for w in range(shaped))),
+                ),
+            ],
+            axis=2,
+        )
+        t1 = 2 * t1
+    shard_piece = jnp.roll(all_values, right_arr * ready, axis=2)
     outputs_here = shard_piece.shape[2]
     kernel = shard_piece.reshape(3, 3, 3 * channels, outputs_here)
     summed = jnp.zeros((frames, rows_here, columns, outputs_here), jnp.float32)

time: 210 us -> 347 us (1.65)
  waiting for transfers between devices: 104 us -> 232 us
  other arithmetic: 18.6 us -> 34.2 us
  between operations: 13.8 us -> 0.45 us
    ppermute x0 -> x6, waiting for transfers between devices: none -> 148 us  [convolve(): lax.ppermute(all_values, ('tm', 'tile'), tuple(((w, (w - t1) % shaped) fo...]
    ppermute x2, waiting for transfers between devices: 94.4 us -> 77.2 us  [from_behind(): lax.ppermute(value, axis, [(source, source + steps) for source in range(f...]
    concatenate x0 -> x5, other arithmetic: none -> 15.6 us  [the longest x1 11.1 us: convolve(): shard_piece = jnp.roll(all_values, right_arr * ready, axis=2)]
    all_gather x2 -> x0, local copies, waits for them, and re-layouts: 11.5 us -> none  [convolve(): lax.all_gather(weight_shard, ('tm', 'tile'), axis=2, tiled=True)]
    dynamic_slice x0 -> x2, local copies, waits for them, and re-layouts: none -> 10.6 us  [convolve(): shard_piece = jnp.roll(all_values, right_arr * ready, axis=2)]
    ppermute x0 -> x6, starting transfers between devices: none -> 5.81 us  [convolve(): lax.ppermute(all_values, ('tm', 'tile'), tuple(((w, (w - t1) % shaped) fo...]
  transfers between devices with their start and end apart: 8 -> 12, of which waited for: 5 -> 9; matrix products, arithmetic and copies ran while one was open for 20% -> 6% of each run, Pallas kernels for 0% -> 0%
where the time goes in v1:
time: 347 us; the launch traced here: 346 us
  waiting for transfers between devices  232 us (67%)
  other arithmetic  34.2 us (10%)
  matrix products  26.9 us (8%)
  blocking collectives  19.7 us (6%)
  local copies, waits for them, and re-layouts  17.6 us (5%)
  starting transfers between devices  15.2 us (4%)
    ppermute x6, waiting for transfers between devices, convolve(): lax.ppermute(all_values, ('tm', 'tile'), tuple(((w, (w - t1) % shaped) fo...  148 us
    ppermute x2, waiting for transfers between devices, from_behind(): lax.ppermute(value, axis, [(source, source + steps) for source in range(f...  77.2 us
    dot_general x18, matrix products, convolve(): jnp.einsum('trwk,kn->trwn', widened[frame_off:frame_off + frames, row_off...  26.9 us
    concatenate x1, other arithmetic, convolve(): shard_piece = jnp.roll(all_values, right_arr * ready, axis=2)  11.1 us
    dynamic_slice x2, local copies, waits for them, and re-layouts, convolve(): shard_piece = jnp.roll(all_values, right_arr * ready, axis=2)  10.6 us
    psum x2, blocking collectives, normalize(): spread = lax.psum(jnp.sum(centered * centered, axis=(1, 3)), 'tile')  9.85 us
    psum x2, blocking collectives, normalize(): totals = lax.psum(jnp.sum(grouped, axis=(1, 3)), 'tile')  9.85 us
  transfers between devices with their start and end apart: 12, of which 9 were waited for; matrix products, arithmetic and copies ran while one was open for 6% of the time, Pallas kernels for 0%

profile of v1, /device:TPU:24, one launch (start us, length us, event | category | flops | bytes accessed | tf_op | source)
XLA Modules:
  0.0 345.9 jit_solution(9620271870141404566)
XLA Ops:
  0.0 1.5 convert_reduce_fusion
  1.7 4.9 %psum.28 = f32[2,32]{1,0:T(2,128)S(1)} all-reduce(f32[2,32]{1,0:T(2,128)S(1)} %reduce_sum.51), channel_id=1, replica_groups=mesh['tm'=4,'tile'=2,'clip'=4] {'tile'}, use_global_device_ids=true, to_apply=%region_2.0 | all-reduce | flops 64 | bytes 512 | tf_op jit(solution)/shard_map/psum | solution.py:33
  6.8 1.5 fusion.29
  8.5 4.9 %psum.29 = f32[2,32]{1,0:T(2,128)S(1)} all-reduce(f32[2,32]{1,0:T(2,128)S(1)} %reduce_sum.54), channel_id=1, replica_groups=mesh['tm'=4,'tile'=2,'clip'=4] {'tile'}, use_global_device_ids=true, to_apply=%region_5.6 | all-reduce | flops 64 | bytes 512 | tf_op jit(solution)/shard_map/psum | solution.py:36
  13.6 1.9 fusion.36
  16.8 3.7 %collective-permute-start.3 = (bf16[27,256,32]{1,2,0:T(8,128)(2,1)S(1)}, bf16[27,256,32]{1,2,0:T(8,128)(2,1)S(1)}, u32[]{:S(2)}, u32[]{:S(2)}) collective-permute-start(bf16[27,256,32]{1,2,0:T(8,128)(2,1)S(1)} %copy-done.3), channel_id=1, source_target_pairs={{0,28},{4,0},{8,4},{12,8},{16,12},{20,16},{24,20},{28,24},{1,29},{... | collective-permute-start | bytes 1327112 | tf_op jit(solution)/shard_map/ppermute | solution.py:63
  20.9 10.1 %collective-permute-done.3 = bf16[27,256,32]{1,2,0:T(8,128)(2,1)S(1)} collective-permute-done((bf16[27,256,32]{1,2,0:T(8,128)(2,1)S(1)}, bf16[27,256,32]{1,2,0:T(8,128)(2,1)S(1)}, u32[]{:S(2)}, u32[]{:S(2)}) %collective-permute-start.3) | collective-permute-done | bytes 442400 | tf_op jit(solution)/shard_map/ppermute | solution.py:63
  32.1 1.5 collective-permute-start.4
  33.6 53.8 %collective-permute-done = bf16[2,8,128,256]{3,2,1,0:T(8,128)(2,1)S(1)} collective-permute-done((bf16[2,8,128,256]{3,2,1,0:T(8,128)(2,1)S(1)}, bf16[2,8,128,256]{3,2,1,0:T(8,128)(2,1)S(1)}, u32[]{:S(2)}, u32[]{:S(2)}) %collective-permute-start) | collective-permute-done | bytes 1048608 | tf_op jit(solution)/shard_map/ppermute | solution.py:13
  88.2 2.0 collective-permute-start.1
  93.7 5.1 %collective-permute-done.2 = bf16[4,1,128,256]{3,2,1,0:T(8,128)(2,1)} collective-permute-done((bf16[4,1,128,256]{3,2,1,0:T(8,128)(2,1)}, bf16[4,1,128,256]{3,2,1,0:T(8,128)(2,1)}, u32[]{:S(2)}, u32[]{:S(2)}) %collective-permute-start.2) | collective-permute-done | bytes 262176 | tf_op jit(solution)/shard_map/ppermute | solution.py:24
  98.8 2.1 fusion.22
  102.4 15.7 %collective-permute-done.10 = bf16[27,256,64]{1,2,0:T(8,128)(2,1)} collective-permute-done((bf16[27,256,64]{1,2,0:T(8,128)(2,1)}, bf16[27,256,64]{1,2,0:T(8,128)(2,1)}, u32[]{:S(2)}, u32[]{:S(2)}) %collective-permute-start.10) | collective-permute-done | bytes 884768 | tf_op jit(solution)/shard_map/ppermute | solution.py:63
  119.4 1.9 fusion.63
  121.3 4.8 %pad_maximum_fusion = bf16[4,10,128,768]{3,2,1,0:T(8,128)(2,1)} fusion(bf16[4,10,128,256]{3,2,1,0:T(8,128)(2,1)S(1)} %get-tuple-element.9, bf16[4,1,128,256]{3,2,1,0:T(8,128)(2,1)} %collective-permute-done.2, bf16[2,8,128,256]{3,2,1,0:T(8,128)(2,1)S(1)} %fusion.36, bf16[2,8,128,256]{3,2,1,0:T(8,128)(2,1)S(1)} %collective-permute-done, ...), kind=kLoop, calls=%fused_computation.2 | loop fusion | flops 47185920 | bytes 15728640 | tf_op jit(solution)/shard_map/concatenate | solution.py:46
  126.1 84.4 %collective-permute-done.5 = bf16[27,256,128]{1,2,0:T(8,128)(2,1)S(1)} collective-permute-done((bf16[27,256,128]{1,2,0:T(8,128)(2,1)S(1)}, bf16[27,256,128]{1,2,0:T(8,128)(2,1)S(1)}, u32[]{:S(2)}, u32[]{:S(2)}) %collective-permute-start.5) | collective-permute-done | bytes 1769504 | tf_op jit(solution)/shard_map/ppermute | solution.py:63
  210.5 37.9 %collective-permute-done.11 = bf16[27,256,128]{1,2,0:T(8,128)(2,1)S(1)} collective-permute-done((bf16[27,256,128]{1,2,0:T(8,128)(2,1)S(1)}, bf16[27,256,128]{1,2,0:T(8,128)(2,1)S(1)}, u32[]{:S(2)}, u32[]{:S(2)}) %collective-permute-start.11) | collective-permute-done | bytes 1769504 | tf_op jit(solution)/shard_map/ppermute | solution.py:63
  248.4 11.1 %fusion.4 = (bf16[27,256,256]{1,2,0:T(8,128)(2,1)}, bf16[27,256,256]{1,2,0:T(8,128)(2,1)}) fusion(s32[]{:T(128)S(6)} %select_n.13, bf16[27,256,32]{1,2,0:T(8,128)(2,1)S(1)} %copy-done.2, bf16[27,256,32]{1,2,0:T(8,128)(2,1)S(1)} %copy-done.5, bf16[27,256,64]{1,2,0:T(8,128)(2,1)} %collective-permute-done.10, ...), kind=kLoop, calls=%fused_computation.24 | loop fusion | flops 56623104 | bytes 14155780 | tf_op jit(solution)/shard_map/jit(_roll_dynamic)/concatenate | solution.py:72
  259.5 4.6 %copy.10 = bf16[27,256,256]{2,1,0:T(8,128)(2,1)S(1)} copy(bf16[27,256,256]{1,2,0:T(8,128)(2,1)} %get-tuple-element.17) | data formatting | bytes 7077888 | tf_op jit(solution)/shard_map/jit(_roll_dynamic)/dynamic_slice | solution.py:72
  264.2 3.1 fusion.54
  267.2 3.1 fusion.55
  270.3 2.9 fusion.56
  278.3 2.5 convert_reduce_fusion.1
  280.9 4.9 %psum.30 = f32[2,32]{1,0:T(2,128)S(1)} all-reduce(f32[2,32]{1,0:T(2,128)S(1)} %reduce_sum.72), channel_id=1, replica_groups=mesh['tm'=4,'tile'=2,'clip'=4] {'tile'}, use_global_device_ids=true, to_apply=%region_8.10 | all-reduce | flops 64 | bytes 512 | tf_op jit(solution)/shard_map/psum | solution.py:33
  286.0 1.5 fusion.37
  287.7 4.9 %psum.31 = f32[2,32]{1,0:T(2,128)S(1)} all-reduce(f32[2,32]{1,0:T(2,128)S(1)} %reduce_sum.75), channel_id=1, replica_groups=mesh['tm'=4,'tile'=2,'clip'=4] {'tile'}, use_global_device_ids=true, to_apply=%region_11.13 | all-reduce | flops 64 | bytes 512 | tf_op jit(solution)/shard_map/psum | solution.py:36
  292.8 1.9 fusion.44
  296.0 23.5 %collective-permute-done.6 = bf16[2,8,128,256]{3,2,1,0:T(8,128)(2,1)S(1)} collective-permute-done((bf16[2,8,128,256]{3,2,1,0:T(8,128)(2,1)S(1)}, bf16[2,8,128,256]{3,2,1,0:T(8,128)(2,1)S(1)}, u32[]{:S(2)}, u32[]{:S(2)}) %collective-permute-start.6) | collective-permute-done | bytes 1048608 | tf_op jit(solution)/shard_map/ppermute | solution.py:13
  319.6 2.2 collective-permute-start.7
  323.0 5.9 %copy.11 = bf16[27,256,256]{2,1,0:T(8,128)(2,1)} copy(bf16[27,256,256]{1,2,0:T(8,128)(2,1)} %get-tuple-element.16) | data formatting | bytes 7077888 | tf_op jit(solution)/shard_map/jit(_roll_dynamic)/dynamic_slice | solution.py:72
  331.3 1.9 fusion.62
  343.3 2.6 fusion.45
  (77 shorter events, 31.2 us)
Async XLA Ops:
  0.0 16.8 %copy-start.3 = (bf16[27,256,32]{1,2,0:T(8,128)(2,1)S(1)}, bf16[27,256,32]{1,2,0:T(8,128)(2,1)}, u32[]{:S(2)}) copy-start(bf16[27,256,32]{1,2,0:T(8,128)(2,1)} %param.11) | copy-start | bytes 1327108
  0.0 20.4 %copy-start.2 = (bf16[27,256,32]{1,2,0:T(8,128)(2,1)S(1)}, bf16[27,256,32]{1,2,0:T(8,128)(2,1)}, u32[]{:S(2)}) copy-start(bf16[27,256,32]{1,2,0:T(8,128)(2,1)} %param.14) | copy-start | bytes 1327108
  15.5 71.9 %collective-permute-start = (bf16[2,8,128,256]{3,2,1,0:T(8,128)(2,1)S(1)}, bf16[2,8,128,256]{3,2,1,0:T(8,128)(2,1)S(1)}, u32[]{:S(2)}, u32[]{:S(2)}) collective-permute-start(bf16[2,8,128,256]{3,2,1,0:T(8,128)(2,1)S(1)} %fusion.36), channel_id=1, source_target_pairs={{0,8},{8,16},{16,24},{1,9},{9,17},{17,25},{2,10},{10,18},{18,26},{... | collective-permute-start | bytes 3145736 | tf_op jit(solution)/shard_map/ppermute | solution.py:13
  16.8 14.3 %collective-permute-start.3 = (bf16[27,256,32]{1,2,0:T(8,128)(2,1)S(1)}, bf16[27,256,32]{1,2,0:T(8,128)(2,1)S(1)}, u32[]{:S(2)}, u32[]{:S(2)}) collective-permute-start(bf16[27,256,32]{1,2,0:T(8,128)(2,1)S(1)} %copy-done.3), channel_id=1, source_target_pairs={{0,28},{4,0},{8,4},{12,8},{16,12},{20,16},{24,20},{28,24},{1,29},{... | collective-permute-start | bytes 1327112 | tf_op jit(solution)/shard_map/ppermute | solution.py:63
  20.5 71.1 %collective-permute-start.9 = (bf16[27,256,32]{1,2,0:T(8,128)(2,1)S(1)}, bf16[27,256,32]{1,2,0:T(8,128)(2,1)S(1)}, u32[]{:S(2)}, u32[]{:S(2)}) collective-permute-start(bf16[27,256,32]{1,2,0:T(8,128)(2,1)S(1)} %copy-done.2), channel_id=1, source_target_pairs={{0,28},{4,0},{8,4},{12,8},{16,12},{20,16},{24,20},{28,24},{1,29},{... | collective-permute-start | bytes 1327112 | tf_op jit(solution)/shard_map/ppermute | solution.py:63
  32.1 68.9 %collective-permute-start.4 = (bf16[27,256,64]{1,2,0:T(8,128)(2,1)}, bf16[27,256,64]{1,2,0:T(8,128)(2,1)}, u32[]{:S(2)}, u32[]{:S(2)}) collective-permute-start(bf16[27,256,64]{1,2,0:T(8,128)(2,1)} %pad_maximum_fusion.4), channel_id=1, source_target_pairs={{0,24},{4,28},{8,0},{12,4},{16,8},{20,12},{24,16},{28,20},{1,25},{... | collective-permute-start | bytes 2654216 | tf_op jit(solution)/shard_map/ppermute | solution.py:63
  88.2 5.5 %collective-permute-start.1 = (bf16[4,1,128,256]{3,2,1,0:T(8,128)(2,1)}, bf16[4,1,128,256]{3,2,1,0:T(8,128)(2,1)}, u32[]{:S(2)}, u32[]{:S(2)}) collective-permute-start(bf16[4,1,128,256]{3,2,1,0:T(8,128)(2,1)} %get-tuple-element.12), channel_id=1, source_target_pairs={{0,4},{1,5},{2,6},{3,7},{8,12},{9,13},{10,14},{11,15},{16,20},{17,... | collective-permute-start | bytes 786440 | tf_op jit(solution)/shard_map/ppermute | solution.py:21
  90.2 8.6 %collective-permute-start.2 = (bf16[4,1,128,256]{3,2,1,0:T(8,128)(2,1)}, bf16[4,1,128,256]{3,2,1,0:T(8,128)(2,1)}, u32[]{:S(2)}, u32[]{:S(2)}) collective-permute-start(bf16[4,1,128,256]{3,2,1,0:T(8,128)(2,1)} %get-tuple-element.13), channel_id=1, source_target_pairs={{4,0},{5,1},{6,2},{7,3},{12,8},{13,9},{14,10},{15,11},{20,16},{21,... | collective-permute-start | bytes 786440 | tf_op jit(solution)/shard_map/ppermute | solution.py:24
  91.5 0.8 copy-start.4
  93.3 24.8 %collective-permute-start.10 = (bf16[27,256,64]{1,2,0:T(8,128)(2,1)}, bf16[27,256,64]{1,2,0:T(8,128)(2,1)}, u32[]{:S(2)}, u32[]{:S(2)}) collective-permute-start(bf16[27,256,64]{1,2,0:T(8,128)(2,1)} %pad_maximum_fusion.5), channel_id=1, source_target_pairs={{0,24},{4,28},{8,0},{12,4},{16,8},{20,12},{24,16},{28,20},{1,25},{... | collective-permute-start | bytes 2654216 | tf_op jit(solution)/shard_map/ppermute | solution.py:63
  93.3 24.8 %copy-start.5 = (bf16[27,256,32]{1,2,0:T(8,128)(2,1)S(1)}, bf16[27,256,32]{1,2,0:T(8,128)(2,1)}, u32[]{:S(2)}) copy-start(bf16[27,256,32]{1,2,0:T(8,128)(2,1)} %copy-done.4) | copy-start | bytes 1327108
  102.3 108.2 %collective-permute-start.5 = (bf16[27,256,128]{1,2,0:T(8,128)(2,1)S(1)}, bf16[27,256,128]{1,2,0:T(8,128)(2,1)S(1)}, u32[]{:S(2)}, u32[]{:S(2)}) collective-permute-start(bf16[27,256,128]{1,2,0:T(8,128)(2,1)S(1)} %pad_maximum_fusion.2), channel_id=1, source_target_pairs={{0,16},{4,20},{8,24},{12,28},{16,0},{20,4},{24,8},{28,12},{1,17},{... | collective-permute-start | bytes 5308424 | tf_op jit(solution)/shard_map/ppermute | solution.py:63
  119.4 129.1 %collective-permute-start.11 = (bf16[27,256,128]{1,2,0:T(8,128)(2,1)S(1)}, bf16[27,256,128]{1,2,0:T(8,128)(2,1)S(1)}, u32[]{:S(2)}, u32[]{:S(2)}) collective-permute-start(bf16[27,256,128]{1,2,0:T(8,128)(2,1)S(1)} %pad_maximum_fusion.3), channel_id=1, source_target_pairs={{0,16},{4,20},{8,24},{12,28},{16,0},{20,4},{24,8},{28,12},{1,17},{... | collective-permute-start | bytes 5308424 | tf_op jit(solution)/shard_map/ppermute | solution.py:63
  264.2 9.1 %slice-start = ((s8[7864320]{0:T(1024)(128)(4,1)}), s8[4194304]{0:T(1024)(128)(4,1)S(1)}, s32[]{:S(2)}) async-start(s8[7864320]{0:T(1024)(128)(4,1)} %bitcast.148), calls=%async_computation | async-start | bytes 8388608
  267.2 6.0 %slice-start.1 = ((s8[7864320]{0:T(1024)(128)(4,1)}), s8[3670016]{0:T(1024)(128)(4,1)S(1)}, s32[]{:S(2)}) async-start(s8[7864320]{0:T(1024)(128)(4,1)} %bitcast.148), calls=%async_computation.1 | async-start | bytes 7340032
  277.2 1.0 copy-start.6
  278.2 14.6 %copy-start.8 = (f32[256]{0:T(256)S(1)}, f32[256]{0:T(256)}, u32[]{:S(2)}) copy-start(f32[256]{0:T(256)} %param.13) | copy-start | bytes 3076
  294.7 24.8 %collective-permute-start.6 = (bf16[2,8,128,256]{3,2,1,0:T(8,128)(2,1)S(1)}, bf16[2,8,128,256]{3,2,1,0:T(8,128)(2,1)S(1)}, u32[]{:S(2)}, u32[]{:S(2)}) collective-permute-start(bf16[2,8,128,256]{3,2,1,0:T(8,128)(2,1)S(1)} %fusion.44), channel_id=1, source_target_pairs={{0,8},{8,16},{16,24},{1,9},{9,17},{17,25},{2,10},{10,18},{18,26},{... | collective-permute-start | bytes 3145736 | tf_op jit(solution)/shard_map/ppermute | solution.py:13
  319.6 9.4 %collective-permute-start.7 = (bf16[4,1,128,256]{3,2,1,0:T(8,128)(2,1)S(1)}, bf16[4,1,128,256]{3,2,1,0:T(8,128)(2,1)S(1)}, u32[]{:S(2)}, u32[]{:S(2)}) collective-permute-start(bf16[4,1,128,256]{3,2,1,0:T(8,128)(2,1)S(1)} %get-tuple-element.10), channel_id=1, source_target_pairs={{0,4},{1,5},{2,6},{3,7},{8,12},{9,13},{10,14},{11,15},{16,20},{17,... | collective-permute-start | bytes 786440 | tf_op jit(solution)/shard_map/ppermute | solution.py:21
  321.7 8.3 %collective-permute-start.8 = (bf16[4,1,128,256]{3,2,1,0:T(8,128)(2,1)S(1)}, bf16[4,1,128,256]{3,2,1,0:T(8,128)(2,1)S(1)}, u32[]{:S(2)}, u32[]{:S(2)}) collective-permute-start(bf16[4,1,128,256]{3,2,1,0:T(8,128)(2,1)S(1)} %get-tuple-element.11), channel_id=1, source_target_pairs={{4,0},{5,1},{6,2},{7,3},{12,8},{13,9},{14,10},{15,11},{20,16},{21,... | collective-permute-start | bytes 786440 | tf_op jit(solution)/shard_map/ppermute | solution.py:24
  333.1 2.0 copy-start.1
  342.1 1.2 copy-start
  342.1 1.2 copy-start.7
